TPU v7x, 32 devices: a whole 2x2x4 slice. The times are simulated.
32 devices in a mesh: date: 2 (over y), trade: 8 (over z, x), path: 2 (over core).
Axes of the slice: x: 2, y: 2, z: 4, core: 2. Of those that a mesh axis runs over, the one named last changes fastest.
Arguments:
- basis_values: bfloat16 [2048, 512], P(('date', 'path')), parts along dimension 0, may hold values from -6 to 6
- coefficients: bfloat16 [2560, 512], P(('date', 'trade')), parts along dimension 0, may hold values from -0.25 to 0.25
- trade_cpty: int32 [1280], P('trade'), may hold values from 0 to 127, as said below
- trade_bucket: int32 [1280], P('trade'), may hold values from 0 to 127
- risk_weights: float32 [128], replicated, may hold values from 0.5 to 2
- correlation: float32 [128, 128], replicated, may hold values from 0 to 1, as said below
- funding_spread: float32 [128], P('trade'), may hold values from 0.5 to 2
Outputs:
- margin: float32 [128, 2048], P('trade', ('date', 'path')), parts along dimension 1
- basis_adjoint: bfloat16 [2048, 512], P(('date', 'path')), parts along dimension 0
There are 2 independent parts, one for each index of `date`. A program takes and returns all parts, laid end to end along the dimension named above; an argument that names none is the same for every part. Nothing has to cross between parts.
Inputs may be any that keep to these rules, and one draw needn't show every extreme that they name: `trade_cpty`: counterparty c belongs to owner block c // 16. Among the trades of one device, at most 40 belong to counterparties of one owner block; in every draw one owner block receives exactly 40 from every device. Counterparties differ in size. `correlation`: symmetric positive definite with unit diagonal; smallest eigenvalue at least 0.01; entries positive.
All inputs are finite; a program needn't handle non-finite values.
Results may differ from a plain program's by a relative error of at most 0.0034.
Values may be sent and summed in bfloat16 or wider, within the bound.
No kernel may reach another device: no remote copies, remote signals or barrier semaphores. Data moves between devices by JAX's collectives and lax.ppermute only.
A program may use at most 64 MiB of HBM per device.

v0:
```python
import jax
import jax.numpy as jnp
from jax import lax
from jax.sharding import PartitionSpec as P


def margin_terms(arrived, got_codes, risk_weights, correlation, funding_spread):
    path_rows = arrived.shape[0]
    cpty_count = funding_spread.shape[0]
    bucket_count = risk_weights.shape[0]
    is_filled = got_codes >= 0
    column_ids = jnp.arange(cpty_count * bucket_count, dtype=jnp.int32)
    hot_table = (got_codes[:, None] == column_ids[None, :]).astype(jnp.bfloat16)
    bucket_sums = jnp.dot(arrived, hot_table, preferred_element_type=jnp.float32)
    weighted = (
        bucket_sums.reshape(path_rows, cpty_count, bucket_count) * risk_weights[None, None, :]
    )
    rho_w = jnp.einsum("pcb,db->pcd", weighted, correlation, precision=lax.Precision.HIGHEST)
    margin_now = jnp.sqrt(jnp.sum(weighted * rho_w, axis=2) + 1e-06)
    sens_bar = (
        funding_spread[None, :, None] * risk_weights[None, None, :] * rho_w / margin_now[:, :, None]
    )
    flat_bar = sens_bar.reshape(path_rows, cpty_count * bucket_count)
    safe_codes = jnp.where(is_filled, got_codes, 0)
    slot_bar = jnp.take(flat_bar, safe_codes, axis=1) * is_filled[None, :].astype(jnp.float32)
    return (margin_now, slot_bar.astype(jnp.bfloat16))


def body(
    basis_values, coefficients, trade_cpty, trade_bucket, risk_weights, correlation, funding_spread
):
    owners = lax.axis_size("trade")
    per_device = coefficients.shape[0]
    capacity = max(2, 2 * per_device // owners)
    slot_total = owners * capacity
    cpty_count = funding_spread.shape[0]
    bucket_count = risk_weights.shape[0]
    path_rows = basis_values.shape[0]
    owner_of = trade_cpty // cpty_count
    trade_code = trade_cpty % cpty_count * bucket_count + trade_bucket
    position = jnp.arange(per_device, dtype=jnp.int32)
    same_owner = owner_of[:, None] == owner_of[None, :]
    earlier = position[None, :] < position[:, None]
    rank_in = jnp.sum((same_owner & earlier).astype(jnp.int32), axis=1)
    slot_index = owner_of * capacity + rank_in
    codes_out = jnp.full((slot_total,), -1, jnp.int32).at[slot_index].set(trade_code)
    got_codes = lax.all_to_all(codes_out, "trade", split_axis=0, concat_axis=0, tiled=True)
    delta_rows = lax.dot_general(
        basis_values, coefficients, (((1,), (1,)), ((), ())), preferred_element_type=jnp.float32
    ).astype(jnp.bfloat16)
    outgoing = jnp.zeros((path_rows, slot_total), jnp.bfloat16).at[:, slot_index].set(delta_rows)
    arrived = lax.all_to_all(outgoing, "trade", split_axis=1, concat_axis=1, tiled=True)
    margin_now, slot_bar = margin_terms(
        arrived, got_codes, risk_weights, correlation, funding_spread
    )
    returned = lax.all_to_all(slot_bar, "trade", split_axis=1, concat_axis=1, tiled=True)
    delta_bar = returned[:, slot_index]
    partial_adj = jnp.dot(delta_bar, coefficients, preferred_element_type=jnp.float32)
    basis_adjoint = lax.psum(partial_adj, "trade").astype(jnp.bfloat16)
    return (margin_now.T, basis_adjoint)


def solution(mesh):
    placed = (
        P(("date", "path"), None),
        P(("date", "trade"), None),
        P("trade"),
        P("trade"),
        P(),
        P(),
        P("trade"),
    )
    return jax.shard_map(
        body,
        mesh=mesh,
        in_specs=placed,
        out_specs=(P("trade", ("date", "path")), P(("date", "path"), None)),
        check_vma=False,
    )
```

profile of v0, /device:TPU:0, one launch (start us, length us, event | category | flops | bytes accessed | tf_op | source)
XLA Modules:
  0.0 130.3 jit_solution(14144373721821639996)
XLA Ops:
  0.6 0.0 copy-start
  0.6 0.8 fusion.14
  1.4 0.2 convert_reduce_fusion
  1.6 1.1 scatter_custom_fusion.1
  2.7 0.7 all_to_all.25
  3.4 7.3 %all-to-all-start.1 = ((s32[8,40,1]{1,2,0:T(1,128)}), s32[8,40,1]{1,2,0:T(1,128)S(1)}, u32[]{:S(2)}, u32[]{:S(2)}) async-start(s32[8,40,1]{1,2,0:T(1,128)} %all_to_all.25), calls=%async_computation.1 | async-start | bytes 8192 | tf_op jit(solution)/shard_map/all_to_all | solution.py:47
  10.6 0.0 copy-done
  10.7 1.2 fusion.7
  11.9 0.0 copy-start.2
  11.9 0.0 copy-start.3
  11.9 1.9 %scatter_custom_fusion = bf16[512,320]{0,1:T(8,128)(2,1)} fusion(s32[160]{0:T(256)S(1)} %compare_select_fusion.4, bf16[160,512]{1,0:T(8,128)(2,1)S(1)} %fusion.7, bf16[]{:T(256)} %constant.45.clone.1), kind=kCustom, calls=%fused_computation.18 | custom fusion | bytes 327682 | tf_op jit(solution)/shard_map/scatter | solution.py:51
  13.8 3.2 %all-to-all-done.1 = s32[8,40,1]{1,2,0:T(1,128)S(1)} async-done(((s32[8,40,1]{1,2,0:T(1,128)}), s32[8,40,1]{1,2,0:T(1,128)S(1)}, u32[]{:S(2)}, u32[]{:S(2)}) %all-to-all-start.1) | async-done | bytes 1312 | tf_op jit(solution)/shard_map/all_to_all | solution.py:47
  17.0 3.4 %all-to-all-start = ((bf16[512,8,40]{0,2,1:T(8,128)(2,1)}), bf16[512,8,40]{0,2,1:T(8,128)(2,1)S(1)}, u32[]{:S(2)}, u32[]{:S(2)}) async-start(bf16[512,8,40]{0,2,1:T(8,128)(2,1)} %bitcast.1), calls=%async_computation | async-start | bytes 655360 | tf_op jit(solution)/shard_map/all_to_all | solution.py:52
  20.5 0.7 broadcast_multiply_fusion
  21.2 0.5 broadcast.164
  21.7 0.7 reduce.7
  22.4 0.1 eq.51
  22.5 0.1 all_to_all.27
  22.6 6.9 %all-to-all-done = bf16[512,8,40]{0,2,1:T(8,128)(2,1)S(1)} async-done(((bf16[512,8,40]{0,2,1:T(8,128)(2,1)}), bf16[512,8,40]{0,2,1:T(8,128)(2,1)S(1)}, u32[]{:S(2)}, u32[]{:S(2)}) %all-to-all-start) | async-done | bytes 327712 | tf_op jit(solution)/shard_map/all_to_all | solution.py:52
  29.6 1.4 %fusion.2 = f32[512,16,128]{0,2,1:T(8,128)S(1)} fusion(bf16[512,320,1]{0,1,2:T(8,128)(2,1)S(1)} %bitcast.29, s32[16,128]{1,0:T(8,128)S(1)} %multiply_add_fusion, s32[320]{0:T(512)S(1)} %eq.51), kind=kOutput, calls=%fused_computation.8 | convolution fusion | flops 671744000 | bytes 4531456 | tf_op jit(solution)/shard_map/dot_general | solution.py:14
  30.9 0.0 copy-done.2
  30.9 0.0 copy-done.3
  31.0 5.5 %multiply_reduce_fusion = (f32[512,16]{0,1:T(8,128)S(1)}, f32[512,16,128]{0,2,1:T(8,128)S(1)}) fusion(f32[512,16,128]{0,2,1:T(8,128)S(1)} %fusion.2, f32[128]{0:T(128)S(1)} %copy-done.3, f32[128,128]{1,0:T(8,128)S(1)} %copy-done.2), kind=kOutput, calls=%fused_computation.5 | convolution fusion | flops 1614798848 | bytes 8487424 | tf_op jit(solution)/shard_map/pcb,db->pcd/dot_general | solution.py:18
  36.4 0.6 add_sqrt_fusion
  37.1 2.4 %multiply_divide_fusion = f32[512,16,128]{0,2,1:T(8,128)} fusion(f32[512,16,128]{0,2,1:T(8,128)S(1)} %get-tuple-element.9, f32[512,16]{0,1:T(8,128)S(1)} %get-tuple-element.2, f32[16,128]{1,0:T(8,128)S(1)} %broadcast_multiply_fusion), kind=kLoop, calls=%fused_computation.4 | loop fusion | flops 2097152 | bytes 8429568 | tf_op jit(solution)/shard_map/div | solution.py:21
  39.5 0.0 copy-start.1
  39.5 4.3 %gather_fusion = f32[320,512]{1,0:T(8,128)S(1)} fusion(f32[512,2048]{0,1:T(8,128)} %bitcast.26, s32[1024]{0:T(1024)S(1)} %pad_clamp_fusion.1), kind=kCustom, calls=%fused_computation | custom fusion | bytes 1312000 | tf_op jit(solution)/shard_map/jit(_take)/gather | solution.py:25
  43.8 0.9 multiply_convert_fusion
  44.7 3.6 %all-to-all-start.2 = ((bf16[512,8,40]{0,2,1:T(8,128)(2,1)}), bf16[512,8,40]{0,2,1:T(8,128)(2,1)S(1)}, u32[]{:S(2)}, u32[]{:S(2)}) async-start(bf16[512,8,40]{0,2,1:T(8,128)(2,1)} %multiply_convert_fusion), calls=%async_computation.2 | async-start | bytes 655360 | tf_op jit(solution)/shard_map/all_to_all | solution.py:56
  48.3 9.6 %all-to-all-done.2 = bf16[512,8,40]{0,2,1:T(8,128)(2,1)S(1)} async-done(((bf16[512,8,40]{0,2,1:T(8,128)(2,1)}), bf16[512,8,40]{0,2,1:T(8,128)(2,1)S(1)}, u32[]{:S(2)}, u32[]{:S(2)}) %all-to-all-start.2) | async-done | bytes 327712 | tf_op jit(solution)/shard_map/all_to_all | solution.py:56
  57.9 0.9 gather_fusion.1
  58.8 0.0 copy-done.1
  58.8 0.3 fusion.18
  59.2 71.2 %all-reduce.1 = bf16[512,512]{1,0:T(8,128)(2,1)} all-reduce(f32[512,512]{1,0:T(8,128)S(1)} %fusion.18), channel_id=1, replica_groups=mesh['date'=2,'trade'=8,'path'=2] {'trade'}, use_global_device_ids=true, to_apply=%region_4.5 | all-reduce | flops 262144 | bytes 1572864 | tf_op jit(solution)/shard_map/psum | solution.py:59
  (6 shorter events, 0.1 us)
Async XLA Ops:
  0.6 10.0 %copy-start = (bf16[512,512]{1,0:T(8,128)(2,1)S(1)}, bf16[512,512]{1,0:T(8,128)(2,1)}, u32[]{:S(2)}) copy-start(bf16[512,512]{1,0:T(8,128)(2,1)} %param.7) | copy-start | bytes 1572868
  3.4 13.6 %all-to-all-start.1 = ((s32[8,40,1]{1,2,0:T(1,128)}), s32[8,40,1]{1,2,0:T(1,128)S(1)}, u32[]{:S(2)}, u32[]{:S(2)}) async-start(s32[8,40,1]{1,2,0:T(1,128)} %all_to_all.25), calls=%async_computation.1 | async-start | bytes 8192 | tf_op jit(solution)/shard_map/all_to_all | solution.py:47
  11.9 19.0 %copy-start.2 = (f32[128,128]{1,0:T(8,128)S(1)}, f32[128,128]{1,0:T(8,128)}, u32[]{:S(2)}) copy-start(f32[128,128]{1,0:T(8,128)} %param.12) | copy-start | bytes 196612
  11.9 19.0 %copy-start.3 = (f32[128]{0:T(128)S(1)}, f32[128]{0:T(128)}, u32[]{:S(2)}) copy-start(f32[128]{0:T(128)} %param.11) | copy-start | bytes 1540
  17.0 12.5 %all-to-all-start = ((bf16[512,8,40]{0,2,1:T(8,128)(2,1)}), bf16[512,8,40]{0,2,1:T(8,128)(2,1)S(1)}, u32[]{:S(2)}, u32[]{:S(2)}) async-start(bf16[512,8,40]{0,2,1:T(8,128)(2,1)} %bitcast.1), calls=%async_computation | async-start | bytes 655360 | tf_op jit(solution)/shard_map/all_to_all | solution.py:52
  39.5 19.3 %copy-start.1 = (bf16[160,512]{1,0:T(8,128)(2,1)S(1)}, bf16[160,512]{1,0:T(8,128)(2,1)}, u32[]{:S(2)}) copy-start(bf16[160,512]{1,0:T(8,128)(2,1)} %param.8) | copy-start | bytes 491524
  44.7 13.2 %all-to-all-start.2 = ((bf16[512,8,40]{0,2,1:T(8,128)(2,1)}), bf16[512,8,40]{0,2,1:T(8,128)(2,1)S(1)}, u32[]{:S(2)}, u32[]{:S(2)}) async-start(bf16[512,8,40]{0,2,1:T(8,128)(2,1)} %multiply_convert_fusion), calls=%async_computation.2 | async-start | bytes 655360 | tf_op jit(solution)/shard_map/all_to_all | solution.py:56
where the time goes:
time: 131 us; the launch traced here: 130 us
  blocking collectives  71.2 us (54%)
  waiting for transfers between devices  19.8 us (15%)
  starting transfers between devices  14.3 us (11%)
  local copies, waits for them, and re-layouts  9.56 us (7%)
  matrix products  8.42 us (6%)
  other arithmetic  6.37 us (5%)
    psum x1, blocking collectives, body(): basis_adjoint = lax.psum(partial_adj, 'trade').astype(jnp.bfloat16)  71.2 us
    all_to_all x1, waiting for transfers between devices, body(): lax.all_to_all(slot_bar, 'trade', split_axis=1, concat_axis=1, tiled=True)  9.6 us
    all_to_all x1, starting transfers between devices, body(): lax.all_to_all(codes_out, 'trade', split_axis=0, concat_axis=0, tiled=True)  7.25 us
    all_to_all x1, waiting for transfers between devices, body(): lax.all_to_all(outgoing, 'trade', split_axis=1, concat_axis=1, tiled=True)  6.93 us
    dot_general x1, matrix products, margin_terms(): jnp.einsum('pcb,db->pcd', weighted, correlation, precision=lax.Precision....  5.47 us
    gather x1, local copies, waits for them, and re-layouts, margin_terms(): jnp.take(flat_bar, safe_codes, axis=1)  4.27 us
    all_to_all x1, starting transfers between devices, body(): lax.all_to_all(slot_bar, 'trade', split_axis=1, concat_axis=1, tiled=True)  3.6 us
    all_to_all x1, starting transfers between devices, body(): lax.all_to_all(outgoing, 'trade', split_axis=1, concat_axis=1, tiled=True)  3.43 us
  transfers between devices with their start and end apart: 3, of which 3 were waited for; matrix products, arithmetic and copies ran while one was open for 4% of the time, Pallas kernels for 0%

commit v1 on v0

--- a/solution.py
+++ b/solution.py
@@ -49,7 +49,19 @@
         basis_values, coefficients, (((1,), (1,)), ((), ())), preferred_element_type=jnp.float32
     ).astype(jnp.bfloat16)
     outgoing = jnp.zeros((path_rows, slot_total), jnp.bfloat16).at[:, slot_index].set(delta_rows)
-    arrived = lax.all_to_all(outgoing, "trade", split_axis=1, concat_axis=1, tiled=True)
+    ways, here = (lax.axis_size("trade"), lax.axis_index("trade"))
+    width = outgoing.shape[1] // ways
+    shape = list(outgoing.shape)
+    shape[1] = width
+    height = shape[1]
+    shape[1] = height * ways
+    full = jnp.zeros(shape, outgoing.dtype)
+    for mask in range(ways):
+        part = lax.dynamic_slice_in_dim(outgoing, (here ^ mask) * width, width, axis=1)
+        if mask:
+            part = lax.ppermute(part, "trade", [(d, d ^ mask) for d in range(ways)])
+        full = lax.dynamic_update_slice_in_dim(full, part, (here ^ mask) * height, axis=1)
+    arrived = full
     margin_now, slot_bar = margin_terms(
         arrived, got_codes, risk_weights, correlation, funding_spread
     )

time: 131 us -> 135 us (1.031)
  starting transfers between devices: 14.3 us -> 22.2 us
  waiting for transfers between devices: 19.8 us -> 17.7 us
    ppermute x0 -> x7, starting transfers between devices: none -> 12.8 us  [body(): part = lax.ppermute(part, 'trade', [(d, d ^ mask) for d in range(ways)])]
    all_to_all x1 -> x0, waiting for transfers between devices: 6.93 us -> none  [body(): lax.all_to_all(outgoing, 'trade', split_axis=1, concat_axis=1, tiled=True)]
    all_to_all x1 -> x0, starting transfers between devices: 3.43 us -> none  [body(): lax.all_to_all(outgoing, 'trade', split_axis=1, concat_axis=1, tiled=True)]
    ppermute x0 -> x7, waiting for transfers between devices: none -> 3.37 us  [body(): part = lax.ppermute(part, 'trade', [(d, d ^ mask) for d in range(ways)])]
    all_to_all x1, waiting for transfers between devices: 3.23 us -> 5.65 us  [body(): lax.all_to_all(codes_out, 'trade', split_axis=0, concat_axis=0, tiled=True)]
    all_to_all x1, starting transfers between devices: 7.25 us -> 4.88 us  [body(): lax.all_to_all(codes_out, 'trade', split_axis=0, concat_axis=0, tiled=True)]
    dot_general x1 -> x0, matrix products: 1.37 us -> none  [margin_terms(): jnp.dot(arrived, hot_table, preferred_element_type=jnp.float32)]
    reshape x0 -> x1, matrix products: none -> 1.37 us  [margin_terms(): bucket_sums.reshape(path_rows, cpty_count, bucket_count)]
  transfers between devices with their start and end apart: 3 -> 9, of which waited for: 3 -> 4; matrix products, arithmetic and copies ran while one was open for 4% -> 2% of each run, Pallas kernels for 0% -> 0%
where the time goes in v1:
time: 135 us
  blocking collectives  70.4 us (52%)
  starting transfers between devices  22.2 us (16%)
  waiting for transfers between devices  17.7 us (13%)
  local copies, waits for them, and re-layouts  9.13 us (7%)
  matrix products  8.42 us (6%)
  other arithmetic  6.36 us (5%)
    psum x1, blocking collectives, body(): basis_adjoint = lax.psum(partial_adj, 'trade').astype(jnp.bfloat16)  70.4 us
    ppermute x7, starting transfers between devices, body(): part = lax.ppermute(part, 'trade', [(d, d ^ mask) for d in range(ways)])  12.8 us
    all_to_all x1, waiting for transfers between devices, body(): lax.all_to_all(slot_bar, 'trade', split_axis=1, concat_axis=1, tiled=True)  8.65 us
    all_to_all x1, waiting for transfers between devices, body(): lax.all_to_all(codes_out, 'trade', split_axis=0, concat_axis=0, tiled=True)  5.65 us
    dot_general x1, matrix products, margin_terms(): jnp.einsum('pcb,db->pcd', weighted, correlation, precision=lax.Precision....  5.48 us
    all_to_all x1, starting transfers between devices, body(): lax.all_to_all(codes_out, 'trade', split_axis=0, concat_axis=0, tiled=True)  4.88 us
    all_to_all x1, starting transfers between devices, body(): lax.all_to_all(slot_bar, 'trade', split_axis=1, concat_axis=1, tiled=True)  4.54 us
    gather x1, local copies, waits for them, and re-layouts, margin_terms(): jnp.take(flat_bar, safe_codes, axis=1)  4.27 us
  transfers between devices with their start and end apart: 9, of which 4 were waited for; matrix products, arithmetic and copies ran while one was open for 2% of the time, Pallas kernels for 0%

profile of v1, /device:TPU:0, one launch (start us, length us, event | category | flops | bytes accessed | tf_op | source)
XLA Modules:
  0.0 135.1 jit_solution(14995912710386384085)
XLA Ops:
  0.6 0.0 copy-start
  0.7 0.8 fusion.12
  1.4 0.2 convert_reduce_fusion
  1.6 0.1 copy-done
  1.7 1.2 fusion.5
  3.0 1.3 scatter_custom_fusion
  4.3 0.0 copy-start.2
  4.3 0.0 copy-start.3
  4.3 0.1 constant_dynamic-slice_fusion
  4.4 3.0 %collective-permute-start = (bf16[512,40]{0,1:T(8,128)(2,1)S(1)}, bf16[512,40]{0,1:T(8,128)(2,1)S(1)}, u32[]{:S(2)}, u32[]{:S(2)}) collective-permute-start(bf16[512,40]{0,1:T(8,128)(2,1)S(1)} %get-tuple-element.8), channel_id=1, source_target_pairs={{0,2},{2,0},{4,6},{6,4},{8,10},{10,8},{12,14},{14,12},{1,3},{3,1},... | collective-permute-start | bytes 122888 | tf_op jit(solution)/shard_map/ppermute | solution.py:62
  7.4 1.6 %collective-permute-start.1 = (bf16[512,40]{0,1:T(8,128)(2,1)S(1)}, bf16[512,40]{0,1:T(8,128)(2,1)S(1)}, u32[]{:S(2)}, u32[]{:S(2)}) collective-permute-start(bf16[512,40]{0,1:T(8,128)(2,1)S(1)} %get-tuple-element.7), channel_id=1, source_target_pairs={{0,4},{2,6},{4,0},{6,2},{8,12},{10,14},{12,8},{14,10},{1,5},{3,7},... | collective-permute-start | bytes 122888 | tf_op jit(solution)/shard_map/ppermute | solution.py:62
  9.0 0.0 collective-permute-start.2
  9.0 3.0 %collective-permute-start.3 = (bf16[512,40]{0,1:T(8,128)(2,1)S(1)}, bf16[512,40]{0,1:T(8,128)(2,1)S(1)}, u32[]{:S(2)}, u32[]{:S(2)}) collective-permute-start(bf16[512,40]{0,1:T(8,128)(2,1)S(1)} %get-tuple-element.5), channel_id=1, source_target_pairs={{0,8},{2,10},{4,12},{6,14},{8,0},{10,2},{12,4},{14,6},{1,9},{3,11}... | collective-permute-start | bytes 122888 | tf_op jit(solution)/shard_map/ppermute | solution.py:62
  12.0 1.3 collective-permute-start.4
  13.2 1.1 scatter_custom_fusion.1
  14.3 0.7 all_to_all.14
  15.0 4.9 %all-to-all-start = ((s32[8,40,1]{1,2,0:T(1,128)}), s32[8,40,1]{1,2,0:T(1,128)S(1)}, u32[]{:S(2)}, u32[]{:S(2)}) async-start(s32[8,40,1]{1,2,0:T(1,128)} %all_to_all.14), calls=%async_computation | async-start | bytes 8192 | tf_op jit(solution)/shard_map/all_to_all | solution.py:47
  19.9 0.7 broadcast_multiply_fusion
  20.6 5.6 %all-to-all-done = s32[8,40,1]{1,2,0:T(1,128)S(1)} async-done(((s32[8,40,1]{1,2,0:T(1,128)}), s32[8,40,1]{1,2,0:T(1,128)S(1)}, u32[]{:S(2)}, u32[]{:S(2)}) %all-to-all-start) | async-done | bytes 1312 | tf_op jit(solution)/shard_map/all_to_all | solution.py:47
  26.3 0.1 all_to_all.16
  26.4 0.5 broadcast.154
  26.9 0.7 reduce.7
  27.6 0.1 eq.35
  27.7 0.0 collective-permute-done
  27.7 0.6 collective-permute-start.5
  28.3 0.0 collective-permute-done.1
  28.3 3.3 %collective-permute-start.6 = (bf16[512,40]{0,1:T(8,128)(2,1)S(1)}, bf16[512,40]{0,1:T(8,128)(2,1)S(1)}, u32[]{:S(2)}, u32[]{:S(2)}) collective-permute-start(bf16[512,40]{0,1:T(8,128)(2,1)S(1)} %get-tuple-element.2), channel_id=1, source_target_pairs={{0,14},{2,12},{4,10},{6,8},{8,6},{10,4},{12,2},{14,0},{1,15},{3,13... | collective-permute-start | bytes 122888 | tf_op jit(solution)/shard_map/ppermute | solution.py:62
  31.6 0.0 collective-permute-done.2
  31.7 0.0 collective-permute-done.3
  31.7 0.0 collective-permute-done.4
  31.7 1.8 %collective-permute-done.5 = bf16[512,40]{0,1:T(8,128)(2,1)S(1)} collective-permute-done((bf16[512,40]{0,1:T(8,128)(2,1)S(1)}, bf16[512,40]{0,1:T(8,128)(2,1)S(1)}, u32[]{:S(2)}, u32[]{:S(2)}) %collective-permute-start.5) | collective-permute-done | bytes 40992 | tf_op jit(solution)/shard_map/ppermute | solution.py:62
  33.5 1.5 %collective-permute-done.6 = bf16[512,40]{0,1:T(8,128)(2,1)S(1)} collective-permute-done((bf16[512,40]{0,1:T(8,128)(2,1)S(1)}, bf16[512,40]{0,1:T(8,128)(2,1)S(1)}, u32[]{:S(2)}, u32[]{:S(2)}) %collective-permute-start.6) | collective-permute-done | bytes 40992 | tf_op jit(solution)/shard_map/ppermute | solution.py:62
  35.1 1.4 %fusion.2 = f32[512,2048]{0,1:T(8,128)S(1)} fusion(bf16[512,320]{0,1:T(8,128)(2,1)S(1)} %constant_dynamic-update-slice_fusion, s32[320]{0:T(512)S(1)} %eq.35), kind=kOutput, calls=%fused_computation.9 | convolution fusion | flops 671744000 | bytes 4523264 | tf_op jit(solution)/shard_map/reshape | solution.py:16
  36.5 0.0 copy-done.2
  36.5 0.0 copy-done.3
  36.5 5.5 %multiply_reduce_fusion = (f32[512,16]{0,1:T(8,128)S(1)}, f32[512,16,128]{0,2,1:T(8,128)S(1)}) fusion(f32[128]{0:T(128)S(1)} %copy-done.3, f32[512,2048]{0,1:T(8,128)S(1)} %fusion.2, f32[128,128]{1,0:T(8,128)S(1)} %copy-done.2, f32[512,16,128]{0,2,1:T(8,128)S(1)} %bitcast.24), kind=kOutput, calls=%fused_computation.5 | convolution fusion | flops 1614798848 | bytes 12681728 | tf_op jit(solution)/shard_map/pcb,db->pcd/dot_general | solution.py:18
  42.0 0.6 add_sqrt_fusion
  42.6 2.5 %multiply_divide_fusion = f32[512,16,128]{0,2,1:T(8,128)} fusion(f32[512,16,128]{0,2,1:T(8,128)S(1)} %get-tuple-element.17, f32[512,16]{0,1:T(8,128)S(1)} %get-tuple-element.10, f32[16,128]{1,0:T(8,128)S(1)} %broadcast_multiply_fusion), kind=kLoop, calls=%fused_computation.4 | loop fusion | flops 2097152 | bytes 8429568 | tf_op jit(solution)/shard_map/div | solution.py:21
  45.0 0.0 copy-start.1
  45.0 4.3 %gather_fusion = f32[320,512]{1,0:T(8,128)S(1)} fusion(f32[512,2048]{0,1:T(8,128)} %bitcast.25, s32[1024]{0:T(1024)S(1)} %pad_clamp_fusion.1), kind=kCustom, calls=%fused_computation | custom fusion | bytes 1312000 | tf_op jit(solution)/shard_map/jit(_take)/gather | solution.py:25
  49.3 0.9 multiply_convert_fusion
  50.2 4.5 %all-to-all-start.1 = ((bf16[512,8,40]{0,2,1:T(8,128)(2,1)}), bf16[512,8,40]{0,2,1:T(8,128)(2,1)S(1)}, u32[]{:S(2)}, u32[]{:S(2)}) async-start(bf16[512,8,40]{0,2,1:T(8,128)(2,1)} %multiply_convert_fusion), calls=%async_computation.1 | async-start | bytes 655360 | tf_op jit(solution)/shard_map/all_to_all | solution.py:68
  54.7 8.7 %all-to-all-done.1 = bf16[512,8,40]{0,2,1:T(8,128)(2,1)S(1)} async-done(((bf16[512,8,40]{0,2,1:T(8,128)(2,1)}), bf16[512,8,40]{0,2,1:T(8,128)(2,1)S(1)}, u32[]{:S(2)}, u32[]{:S(2)}) %all-to-all-start.1) | async-done | bytes 327712 | tf_op jit(solution)/shard_map/all_to_all | solution.py:68
  63.4 0.9 gather_fusion.1
  64.3 0.0 copy-done.1
  64.3 0.3 fusion.16
  64.7 70.4 %all-reduce.1 = bf16[512,512]{1,0:T(8,128)(2,1)} all-reduce(f32[512,512]{1,0:T(8,128)S(1)} %fusion.16), channel_id=1, replica_groups=mesh['date'=2,'trade'=8,'path'=2] {'trade'}, use_global_device_ids=true, to_apply=%region_4.5 | all-reduce | flops 262144 | bytes 1572864 | tf_op jit(solution)/shard_map/psum | solution.py:71
  (13 shorter events, 0.1 us)
Async XLA Ops:
  0.6 1.1 copy-start
  4.3 32.2 %copy-start.2 = (f32[128,128]{1,0:T(8,128)S(1)}, f32[128,128]{1,0:T(8,128)}, u32[]{:S(2)}) copy-start(f32[128,128]{1,0:T(8,128)} %param.12) | copy-start | bytes 196612
  4.3 32.2 %copy-start.3 = (f32[128]{0:T(128)S(1)}, f32[128]{0:T(128)}, u32[]{:S(2)}) copy-start(f32[128]{0:T(128)} %param.11) | copy-start | bytes 1540
  4.4 23.3 %collective-permute-start = (bf16[512,40]{0,1:T(8,128)(2,1)S(1)}, bf16[512,40]{0,1:T(8,128)(2,1)S(1)}, u32[]{:S(2)}, u32[]{:S(2)}) collective-permute-start(bf16[512,40]{0,1:T(8,128)(2,1)S(1)} %get-tuple-element.8), channel_id=1, source_target_pairs={{0,2},{2,0},{4,6},{6,4},{8,10},{10,8},{12,14},{14,12},{1,3},{3,1},... | collective-permute-start | bytes 122888 | tf_op jit(solution)/shard_map/ppermute | solution.py:62
  7.4 20.9 %collective-permute-start.1 = (bf16[512,40]{0,1:T(8,128)(2,1)S(1)}, bf16[512,40]{0,1:T(8,128)(2,1)S(1)}, u32[]{:S(2)}, u32[]{:S(2)}) collective-permute-start(bf16[512,40]{0,1:T(8,128)(2,1)S(1)} %get-tuple-element.7), channel_id=1, source_target_pairs={{0,4},{2,6},{4,0},{6,2},{8,12},{10,14},{12,8},{14,10},{1,5},{3,7},... | collective-permute-start | bytes 122888 | tf_op jit(solution)/shard_map/ppermute | solution.py:62
  9.0 22.7 %collective-permute-start.2 = (bf16[512,40]{0,1:T(8,128)(2,1)S(1)}, bf16[512,40]{0,1:T(8,128)(2,1)S(1)}, u32[]{:S(2)}, u32[]{:S(2)}) collective-permute-start(bf16[512,40]{0,1:T(8,128)(2,1)S(1)} %get-tuple-element.6), channel_id=1, source_target_pairs={{0,6},{2,4},{4,2},{6,0},{8,14},{10,12},{12,10},{14,8},{1,7},{3,5},... | collective-permute-start | bytes 122888 | tf_op jit(solution)/shard_map/ppermute | solution.py:62
  9.0 22.7 %collective-permute-start.3 = (bf16[512,40]{0,1:T(8,128)(2,1)S(1)}, bf16[512,40]{0,1:T(8,128)(2,1)S(1)}, u32[]{:S(2)}, u32[]{:S(2)}) collective-permute-start(bf16[512,40]{0,1:T(8,128)(2,1)S(1)} %get-tuple-element.5), channel_id=1, source_target_pairs={{0,8},{2,10},{4,12},{6,14},{8,0},{10,2},{12,4},{14,6},{1,9},{3,11}... | collective-permute-start | bytes 122888 | tf_op jit(solution)/shard_map/ppermute | solution.py:62
  12.0 19.7 %collective-permute-start.4 = (bf16[512,40]{0,1:T(8,128)(2,1)S(1)}, bf16[512,40]{0,1:T(8,128)(2,1)S(1)}, u32[]{:S(2)}, u32[]{:S(2)}) collective-permute-start(bf16[512,40]{0,1:T(8,128)(2,1)S(1)} %get-tuple-element.4), channel_id=1, source_target_pairs={{0,10},{2,8},{4,14},{6,12},{8,2},{10,0},{12,6},{14,4},{1,11},{3,9}... | collective-permute-start | bytes 122888 | tf_op jit(solution)/shard_map/ppermute | solution.py:62
  15.0 11.3 %all-to-all-start = ((s32[8,40,1]{1,2,0:T(1,128)}), s32[8,40,1]{1,2,0:T(1,128)S(1)}, u32[]{:S(2)}, u32[]{:S(2)}) async-start(s32[8,40,1]{1,2,0:T(1,128)} %all_to_all.14), calls=%async_computation | async-start | bytes 8192 | tf_op jit(solution)/shard_map/all_to_all | solution.py:47
  27.7 5.9 %collective-permute-start.5 = (bf16[512,40]{0,1:T(8,128)(2,1)S(1)}, bf16[512,40]{0,1:T(8,128)(2,1)S(1)}, u32[]{:S(2)}, u32[]{:S(2)}) collective-permute-start(bf16[512,40]{0,1:T(8,128)(2,1)S(1)} %get-tuple-element.3), channel_id=1, source_target_pairs={{0,12},{2,14},{4,8},{6,10},{8,4},{10,6},{12,0},{14,2},{1,13},{3,15... | collective-permute-start | bytes 122888 | tf_op jit(solution)/shard_map/ppermute | solution.py:62
  28.3 6.8 %collective-permute-start.6 = (bf16[512,40]{0,1:T(8,128)(2,1)S(1)}, bf16[512,40]{0,1:T(8,128)(2,1)S(1)}, u32[]{:S(2)}, u32[]{:S(2)}) collective-permute-start(bf16[512,40]{0,1:T(8,128)(2,1)S(1)} %get-tuple-element.2), channel_id=1, source_target_pairs={{0,14},{2,12},{4,10},{6,8},{8,6},{10,4},{12,2},{14,0},{1,15},{3,13... | collective-permute-start | bytes 122888 | tf_op jit(solution)/shard_map/ppermute | solution.py:62
  45.0 19.3 %copy-start.1 = (bf16[160,512]{1,0:T(8,128)(2,1)S(1)}, bf16[160,512]{1,0:T(8,128)(2,1)}, u32[]{:S(2)}) copy-start(bf16[160,512]{1,0:T(8,128)(2,1)} %param.8) | copy-start | bytes 491524
  50.2 13.2 %all-to-all-start.1 = ((bf16[512,8,40]{0,2,1:T(8,128)(2,1)}), bf16[512,8,40]{0,2,1:T(8,128)(2,1)S(1)}, u32[]{:S(2)}, u32[]{:S(2)}) async-start(bf16[512,8,40]{0,2,1:T(8,128)(2,1)} %multiply_convert_fusion), calls=%async_computation.1 | async-start | bytes 655360 | tf_op jit(solution)/shard_map/all_to_all | solution.py:68
